TPU v7x, 32 devices: a whole 2x2x4 slice. The times are simulated.
32 devices in a mesh: groups: 2 (over x), heads: 16 (over z, y, core).
Axes of the slice: x: 2, y: 2, z: 4, core: 2. Of those that a mesh axis runs over, the one named last changes fastest.
Arguments:
- tokens: bfloat16 [64, 4, 2304], P('groups'), parts along dimension 0, may hold values from -6 to 6
- qkv_weight: bfloat16 [4608, 12288], P(('groups', 'heads')), parts along dimension 0, may hold values from -0.125 to 0.125
- gate_weight: bfloat16 [4608, 64], P(('groups', 'heads')), parts along dimension 0, may hold values from -0.125 to 0.125
- conv_weight: bfloat16 [8, 12288], P('groups', 'heads'), parts along dimension 0, may hold values from -3 to 3
- delta_state: float32 [64, 32, 128, 128], P(('groups', 'heads')), parts along dimension 0, may hold values from -0.8 to 0.8
- conv_state: float32 [64, 3, 12288], P(('groups', 'heads')), parts along dimension 0, may hold values from -6 to 6
- old_heads: int32 [32], replicated, may hold values from 0 to 31, each once
- new_units: int32 [64], replicated, may hold values from 0 to 63, each once
- slot_of: int32 [64], P('groups'), parts along dimension 0, may hold values from 0 to 31, each once
- lengths: int32 [64], P('groups'), parts along dimension 0, may hold values from 1 to 4, as said below
Outputs:
- readout: bfloat16 [64, 4, 4096], P('groups', None, 'heads'), parts along dimension 0
There are 2 independent parts, one for each index of `groups`. A program takes and returns all parts, laid end to end along the dimension named above; an argument that names none is the same for every part. Nothing has to cross between parts.
Inputs may be any that keep to these rules, and one draw needn't show every extreme that they name: `old_heads`: a permutation of the heads; old column slot p holds head old_heads[p]. `new_units`: a permutation of the head units; unit u is the half u % 2 of the values of head u // 2. `slot_of`: a permutation of the rows. `lengths`: some row decodes all 4 steps and some row only one.
All inputs are finite; a program needn't handle non-finite values.
Results may differ from a plain program's by a relative error of at most 0.001.
Values may be sent and summed in bfloat16 or wider, within the bound.
A program may use at most 128 MiB of HBM per device.

v0:
```python
import jax
import jax.numpy as jnp
from jax import lax
from jax.sharding import PartitionSpec as P

D = 2304
H = 32
DK = 128
TAPS = 4
STEPS = 4
HALF = 64
UNITS = 64
norm_eps = 1e-06


def unit_tables(old_heads, new_units):
    positions = jnp.arange(H, dtype=jnp.int32)
    inverse = jnp.sum(
        jnp.where(old_heads[None, :] == positions[:, None], positions[None, :], 0), axis=1
    )
    heads_of = new_units // 2
    halves = new_units % 2
    old_slots = jnp.sum(
        jnp.where(heads_of[:, None] == positions[None, :], inverse[None, :], 0), axis=1
    )
    return (old_slots, halves)


def select_units(source, selector, halves, precise):
    lead = source.shape[:-1]
    shaped = source.reshape(lead + (3, H, DK))
    if precise:
        picked = jnp.einsum("...mhk,uh->...muk", shaped, selector, precision=lax.Precision.HIGHEST)
    else:
        picked = jnp.einsum(
            "...mhk,uh->...muk", shaped, selector, preferred_element_type=jnp.float32
        ).astype(source.dtype)
    query_part = picked[..., 0, :, :]
    key_part = picked[..., 1, :, :]
    value_full = picked[..., 2, :, :]
    value_part = jnp.where((halves == 0)[:, None], value_full[..., :HALF], value_full[..., HALF:])
    return jnp.concatenate([query_part, key_part, value_part], axis=-1)


def pick_state(delta_state, selector, halves):
    picked = jnp.einsum("rhkv,uh->rukv", delta_state, selector, precision=lax.Precision.HIGHEST)
    return jnp.where((halves == 0)[None, :, None, None], picked[..., :HALF], picked[..., HALF:])


def normalize(values):
    return values * lax.rsqrt(jnp.sum(values * values, axis=-1, keepdims=True) + norm_eps)


def run_steps(projected, gate_pre, history, tap_weights, carried, live_lengths):
    sequence = jnp.concatenate([history, projected], axis=1)
    weights_f = tap_weights.astype(jnp.float32)
    convolved = weights_f[0][None, None] * sequence[:, 0:STEPS]
    for tap_index in range(1, TAPS):
        convolved = (
            convolved
            + weights_f[tap_index][None, None] * sequence[:, tap_index : tap_index + STEPS]
        )
    activated = jax.nn.silu(convolved)
    queries = normalize(activated[..., :DK])
    keys_all = normalize(activated[..., DK : 2 * DK])
    values_all = activated[..., 2 * DK :]
    beta = jax.nn.sigmoid(gate_pre[..., 0])
    decay = jnp.exp(-jax.nn.softplus(gate_pre[..., 1]))
    readouts = []
    for step_index in range(STEPS):
        is_live = (step_index < live_lengths)[:, None, None, None]
        faded = decay[:, step_index, :, None, None] * carried
        predicted = jnp.sum(keys_all[:, step_index, :, :, None] * faded, axis=2)
        updated = (
            faded
            + beta[:, step_index, :, None, None]
            * keys_all[:, step_index, :, :, None]
            * (values_all[:, step_index] - predicted)[:, :, None, :]
        )
        heads_now = jnp.sum(queries[:, step_index, :, :, None] * updated, axis=2)
        carried = jnp.where(is_live, updated, carried)
        readouts.append(jnp.where(is_live[..., 0], heads_now, jnp.zeros_like(heads_now)))
    return jnp.stack(readouts, axis=1).astype(jnp.bfloat16)


def on_device(
    tokens,
    qkv_weight,
    gate_weight,
    conv_weight,
    delta_state,
    conv_state,
    old_heads,
    new_units,
    slot_of,
    lengths,
):
    devices = lax.axis_size("heads")
    my_index = lax.axis_index("heads")
    per_device = UNITS // devices
    unit_width = 2 * DK + HALF
    old_slots, halves = unit_tables(old_heads, new_units)
    head_range = jnp.arange(H, dtype=jnp.int32)
    selector_bits = old_slots[:, None] == head_range[None, :]
    selector_low = selector_bits.astype(jnp.bfloat16)
    selector_full = selector_bits.astype(jnp.float32)
    local_rows = qkv_weight.shape[0]
    packed = select_units(qkv_weight, selector_low, halves, False).reshape(
        local_rows, devices, per_device, unit_width
    )
    gate_shaped = gate_weight.reshape(local_rows, 2, H)
    packed_gate = jnp.einsum(
        "rmh,uh->rum", gate_shaped, selector_low, preferred_element_type=jnp.float32
    ).astype(jnp.bfloat16)
    packed_gate = packed_gate.reshape(local_rows, devices, per_device, 2)
    mine_weight, mine_gate = (
        lax.all_to_all(packed, "heads", split_axis=1, concat_axis=0, tiled=True),
        lax.all_to_all(packed_gate, "heads", split_axis=1, concat_axis=0, tiled=True),
    )
    row_count = tokens.shape[0]
    row_range = jnp.arange(row_count, dtype=jnp.int32)
    match_rows = slot_of[None, :] == row_range[:, None]
    to_old = match_rows.astype(jnp.bfloat16)
    tokens_old = jnp.einsum(
        "ob,bsd->osd", to_old, tokens, preferred_element_type=jnp.float32
    ).astype(jnp.bfloat16)
    lengths_old = jnp.sum(jnp.where(match_rows, lengths[None, :], 0), axis=1)
    flattened = tokens_old.reshape(row_count * STEPS, D)
    projected = jnp.dot(
        flattened,
        mine_weight.reshape(D, per_device * unit_width),
        preferred_element_type=jnp.float32,
    ).reshape(row_count, STEPS, per_device, unit_width)
    gate_pre = jnp.dot(
        flattened, mine_gate.reshape(D, per_device * 2), preferred_element_type=jnp.float32
    ).reshape(row_count, STEPS, per_device, 2)
    taps_all = lax.all_gather(conv_weight, "heads", axis=1, tiled=True)
    tap_table = select_units(taps_all, selector_low, halves, False)
    rows_dev = delta_state.shape[0]
    got_projected, got_gate = (
        lax.all_to_all(projected, "heads", split_axis=0, concat_axis=2, tiled=True),
        lax.all_to_all(gate_pre, "heads", split_axis=0, concat_axis=2, tiled=True),
    )
    live_lengths = lax.dynamic_slice_in_dim(lengths_old, my_index * rows_dev, rows_dev, 0)
    history = select_units(conv_state, selector_full, halves, True)
    carried = pick_state(delta_state, selector_full, halves)
    local_out = run_steps(got_projected, got_gate, history, tap_table, carried, live_lengths)
    outputs_old = lax.all_to_all(local_out, "heads", split_axis=2, concat_axis=0, tiled=True)
    flat_old = outputs_old.reshape(row_count, STEPS, per_device * HALF)
    outputs = jnp.einsum(
        "ob,osc->bsc", to_old, flat_old, preferred_element_type=jnp.float32
    ).astype(jnp.bfloat16)
    return outputs


def solution(mesh):
    in_specs = (
        P("groups", None, None),
        P(("groups", "heads"), None),
        P(("groups", "heads"), None),
        P("groups", "heads"),
        P(("groups", "heads"), None, None, None),
        P(("groups", "heads"), None, None),
        P(),
        P(),
        P("groups"),
        P("groups"),
    )
    out_specs = P("groups", None, "heads")
    return jax.shard_map(
        on_device, mesh=mesh, in_specs=in_specs, out_specs=out_specs, check_vma=False
    )
```

profile of v0, /device:TPU:0, one launch (start us, length us, event | category | flops | bytes accessed | tf_op | source)
XLA Modules:
  0.0 336.9 jit_solution(10728899009877708103)
XLA Ops:
  0.0 0.7 and_select_fusion.1
  0.7 0.7 select_reduce_fusion.1
  1.6 1.0 fusion.9
  2.5 0.7 copy.168
  3.2 7.4 %all-to-all-start.2 = ((bf16[144,16,4,2]{0,3,2,1:T(2,128)(2,1)}), bf16[144,16,4,2]{0,3,2,1:T(2,128)(2,1)S(1)}, u32[]{:S(2)}, u32[]{:S(2)}) async-start(bf16[144,16,4,2]{0,3,2,1:T(2,128)(2,1)} %bitcast.40), calls=%async_computation.2 | async-start | bytes 131072 | tf_op jit(solution)/shard_map/all_to_all | solution.py:118
  10.7 0.7 fusion.50
  11.3 2.7 copy.172
  14.1 2.0 convert_bitcast_fusion
  16.1 2.5 fusion.52
  18.6 0.8 slice_select_fusion.1
  19.4 6.9 %pad_maximum_fusion = bf16[144,16,4,320]{3,2,1,0:T(4,128)(2,1)} fusion(bf16[144,16,4,64]{3,2,1,0:T(4,128)(2,1)S(1)} %bitcast.162, bf16[144,16,4,128]{3,2,1,0:T(4,128)(2,1)S(1)} %bitcast.161, bf16[144,16,4,128]{3,2,1,0:T(4,128)(2,1)S(1)} %bitcast.160), kind=kLoop, calls=%fused_computation.15 | loop fusion | flops 17694720 | bytes 11796480 | tf_op jit(solution)/shard_map/concatenate | solution.py:42
  26.3 9.1 %copy.167 = bf16[144,16,4,320]{3,2,0,1:T(4,128)(2,1)} copy(bf16[144,16,4,320]{3,2,1,0:T(4,128)(2,1)} %pad_maximum_fusion) | data formatting | bytes 11796480 | tf_op jit(solution)/shard_map/concatenate | solution.py:42
  35.4 6.2 %all-to-all-start = ((bf16[144,16,4,320]{3,2,0,1:T(4,128)(2,1)}), bf16[144,16,4,320]{3,2,0,1:T(4,128)(2,1)}, u32[]{:S(2)}, u32[]{:S(2)}) async-start(bf16[144,16,4,320]{3,2,0,1:T(4,128)(2,1)} %copy.167), calls=%async_computation | async-start | bytes 14155776 | tf_op jit(solution)/shard_map/all_to_all | solution.py:117
  41.6 141.3 %all_gather.3 = bf16[4,12288]{1,0:T(4,128)(2,1)S(1)} all-gather(bf16[4,768]{1,0:T(4,128)(2,1)S(1)} %copy-done.3), channel_id=1, replica_groups=mesh['groups'=2,'heads'=16] {'heads'}, dimensions={1}, use_global_device_ids=true | all-gather | bytes 104448 | tf_op jit(solution)/shard_map/all_gather | solution.py:137
  183.0 0.3 reshape.187
  183.3 0.5 convolution_bitcast_fusion
  184.0 0.4 copy.138
  184.6 0.4 fusion.4
  185.1 0.3 fusion.8
  185.4 11.6 %fusion.5 = f32[2,64,128,128]{3,1,2,0:T(8,128)} fusion(f32[2,32,128,128]{3,2,1,0:T(8,128)} %param.14, s32[64]{0:T(128)S(1)} %select_reduce_fusion), kind=kOutput, calls=%fused_computation.21 | convolution fusion | flops 805308416 | bytes 12583168 | tf_op jit(solution)/shard_map/rhkv,uh->rukv/dot_general | solution.py:46
  197.0 0.1 reshape.192
  197.2 0.5 fusion.24
  197.7 0.8 copy.143
  198.5 27.5 %all-to-all-start.3 = ((f32[32,4,4,2]{2,3,1,0:T(2,128)}), f32[32,4,4,2]{2,3,1,0:T(2,128)S(1)}, u32[]{:S(2)}, u32[]{:S(2)}) async-start(f32[32,4,4,2]{2,3,1,0:T(2,128)} %copy.143), calls=%async_computation.3 | async-start | bytes 262144 | tf_op jit(solution)/shard_map/all_to_all | solution.py:142
  226.0 11.9 %reshape.189 = bf16[2304,1280]{1,0:T(8,128)(2,1)} reshape(bf16[16,144,1,4,320]{4,3,1,0,2:T(4,128)(2,1)} %bitcast.24) | data formatting | bytes 11796480 | tf_op jit(solution)/shard_map/reshape | solution.py:131
  237.8 8.9 %copy.135 = bf16[1280,2304]{1,0:T(8,128)(2,1)} copy(bf16[1280,2304]{0,1:T(8,128)(2,1)} %bitcast.158) | data formatting | bytes 11796480 | tf_op jit(solution)/shard_map/dot_general | solution.py:129
  246.7 4.7 %fusion.58 = f32[32,4,4,320]{3,0,2,1:T(8,128)S(1)} fusion(bf16[32,4,2304,1]{2,0,3,1:T(8,128)(2,1)S(1)} %fusion.4, bf16[4,320,2304,1]{2,1,0,3:T(8,128)(2,1)} %bitcast.163), kind=kOutput, calls=%fused_computation.124 | convolution fusion | flops 754974720 | bytes 7143424 | tf_op jit(solution)/shard_map/dot_general | solution.py:129
  251.5 1.4 copy.136
  252.9 6.0 %all-to-all-start.1 = ((f32[32,4,4,320]{3,2,1,0:T(4,128)}), f32[32,4,4,320]{3,2,1,0:T(4,128)S(1)}, u32[]{:S(2)}, u32[]{:S(2)}) async-start(f32[32,4,4,320]{3,2,1,0:T(4,128)} %copy.136), calls=%async_computation.1 | async-start | bytes 1572864 | tf_op jit(solution)/shard_map/all_to_all | solution.py:141
  259.3 18.3 %all-to-all-done.1 = f32[32,4,4,320]{3,2,1,0:T(4,128)S(1)} async-done(((f32[32,4,4,320]{3,2,1,0:T(4,128)}), f32[32,4,4,320]{3,2,1,0:T(4,128)S(1)}, u32[]{:S(2)}, u32[]{:S(2)}) %all-to-all-start.1) | async-done | bytes 655392 | tf_op jit(solution)/shard_map/all_to_all | solution.py:141
  277.6 0.2 copy.137
  277.8 1.5 divide_multiply_fusion
  279.3 0.3 multiply_reduce_fusion.9
  279.6 0.2 fusion.53
  279.9 0.3 slice_multiply_fusion.1
  280.2 0.2 fusion.55
  281.0 0.2 fusion.54
  282.2 8.5 %multiply_reduce_fusion.7 = (f32[2,64,64]{2,1,0:T(8,128)S(1)}, f32[2,64,128,64]{3,1,2,0:T(8,128)S(1)}) fusion(f32[2,64,128]{1,2,0:T(8,128)S(1)} %copy.148, f32[2,64]{1,0:T(2,128)S(1)} %bitcast.195, f32[2,64,128,128]{3,1,2,0:T(8,128)} %fusion.5, pred[64]{0:T(512)(128)(4,1)S(1)} %fusion.50), kind=kLoop, calls=%fused_computation.12 | loop fusion | flops 4186112 | bytes 12681792 | tf_op jit(solution)/shard_map/reduce_sum | solution.py:73
  290.7 5.1 %multiply_reduce_fusion.5 = f32[2,64,64]{2,1,0:T(8,128)S(1)} fusion(f32[2,64,128,64]{3,1,2,0:T(8,128)S(1)} %get-tuple-element.16, f32[2,64,128]{1,2,0:T(8,128)S(1)} %copy.151, f32[2,64]{1,0:T(2,128)S(1)} %bitcast.202, f32[2,64,64]{2,1,0:T(8,128)S(1)} %sub.35, f32[2,64,128]{1,2,0:T(8,128)S(1)} %copy.147, f32[2,64]{1,0:T(2,128)S(1)} %bitcast.196, ...), kind=kLoop, calls=%fused_computation.9 | loop fusion | flops 7331840 | bytes 4391938 | tf_op jit(solution)/shard_map/reduce_sum | solution.py:73
  295.8 11.4 %multiply_reduce_fusion.6 = (bf16[2,64,64]{2,1,0:T(8,128)(2,1)S(1)}, bf16[2,64,64]{2,1,0:T(8,128)(2,1)S(1)}, f32[2,64,64]{2,1,0:T(8,128)S(1)}, f32[2,64,128,64]{3,1,2,0:T(8,128)S(1)}) fusion(f32[2,64,128,64]{3,1,2,0:T(8,128)S(1)} %get-tuple-element.16, f32[2,64,64]{2,1,0:T(8,128)S(1)} %sub.35, f32[2,64,128]{1,2,0:T(8,128)S(1)} %copy.147, ...), kind=kLoop, calls=%fused_computation.10 | loop fusion | flops 15704064 | bytes 8848900 | tf_op jit(solution)/shard_map/reduce_sum | solution.py:80
  307.3 5.1 %multiply_reduce_fusion.1 = f32[2,64,64]{2,1,0:T(8,128)S(1)} fusion(f32[2,64,128,64]{3,1,2,0:T(8,128)S(1)} %get-tuple-element.18, f32[2,64,128]{1,2,0:T(8,128)S(1)} %copy.157, f32[2,64]{1,0:T(2,128)S(1)} %bitcast.200, f32[2,64,64]{2,1,0:T(8,128)S(1)} %sub.37, f32[2,64,128]{1,2,0:T(8,128)S(1)} %copy.153, f32[2,64]{1,0:T(2,128)S(1)} %bitcast.193, ...), kind=kLoop, calls=%fused_computation.2 | loop fusion | flops 7331840 | bytes 4391938 | tf_op jit(solution)/shard_map/reduce_sum | solution.py:73
  312.4 10.5 %multiply_reduce_fusion.2 = (bf16[2,64,64]{2,1,0:T(8,128)(2,1)S(1)}, bf16[2,64,64]{2,1,0:T(8,128)(2,1)S(1)}) fusion(f32[2,64,128,64]{3,1,2,0:T(8,128)S(1)} %get-tuple-element.18, f32[2,64,64]{2,1,0:T(8,128)S(1)} %sub.37, f32[2,64,128]{1,2,0:T(8,128)S(1)} %copy.153, f32[2,64]{1,0:T(2,128)S(1)} %bitcast.194, f32[2,64,128]{1,2,0:T(8,128)S(1)} %copy.152, ...), kind=kLoop, calls=%fused_computation.4 | loop fusion | flops 11517952 | bytes 4555778 | tf_op jit(solution)/shard_map/reduce_sum | solution.py:80
  323.4 0.1 reshape.202
  323.6 12.1 %all_to_all.81 = bf16[16,2,1024]{2,1,0:T(2,128)(2,1)S(1)} all-to-all(bf16[16,2,1024]{2,1,0:T(2,128)(2,1)S(1)} %reshape.202), channel_id=1, replica_groups=mesh['groups'=2,'heads'=16] {'heads'}, dimensions={0} | all-to-all | bytes 131072 | tf_op jit(solution)/shard_map/all_to_all | solution.py:148
  335.7 0.1 reshape.203
  335.9 0.1 reshape.193
  336.0 0.2 convolution_convert_fusion.2
  336.2 0.7 copy.161
  (65 shorter events, 3.0 us)
Async XLA Ops:
  0.0 184.6 %copy-start = (bf16[32,4,2304]{2,1,0:T(4,128)(2,1)S(1)}, bf16[32,4,2304]{2,1,0:T(4,128)(2,1)}, u32[]{:S(2)}) copy-start(bf16[32,4,2304]{2,1,0:T(4,128)(2,1)} %param.10) | copy-start | bytes 1769476
  3.2 32.2 %all-to-all-start.2 = ((bf16[144,16,4,2]{0,3,2,1:T(2,128)(2,1)}), bf16[144,16,4,2]{0,3,2,1:T(2,128)(2,1)S(1)}, u32[]{:S(2)}, u32[]{:S(2)}) async-start(bf16[144,16,4,2]{0,3,2,1:T(2,128)(2,1)} %bitcast.40), calls=%async_computation.2 | async-start | bytes 131072 | tf_op jit(solution)/shard_map/all_to_all | solution.py:118
  35.4 6.2 %copy-start.3 = (bf16[4,768]{1,0:T(4,128)(2,1)S(1)}, bf16[4,768]{1,0:T(4,128)(2,1)}, u32[]{:S(2)}) copy-start(bf16[4,768]{1,0:T(4,128)(2,1)} %param.13) | copy-start | bytes 18436
  35.4 147.6 %copy-start.2 = (f32[2,3,12288]{2,0,1:T(2,128)S(1)}, f32[2,3,12288]{2,0,1:T(2,128)}, u32[]{:S(2)}) copy-start(f32[2,3,12288]{2,0,1:T(2,128)} %param.15) | copy-start | bytes 884740
  35.4 149.0 %copy-start.4 = (s32[32]{0:T(128)S(1)}, s32[32]{0:T(128)}, u32[]{:S(2)}) copy-start(s32[32]{0:T(128)} %param.18) | copy-start | bytes 388
  35.4 149.0 %copy-start.5 = (s32[32]{0:T(128)S(1)}, s32[32]{0:T(128)}, u32[]{:S(2)}) copy-start(s32[32]{0:T(128)} %param.19) | copy-start | bytes 388
  35.4 163.0 %all-to-all-start = ((bf16[144,16,4,320]{3,2,0,1:T(4,128)(2,1)}), bf16[144,16,4,320]{3,2,0,1:T(4,128)(2,1)}, u32[]{:S(2)}, u32[]{:S(2)}) async-start(bf16[144,16,4,320]{3,2,0,1:T(4,128)(2,1)} %copy.167), calls=%async_computation | async-start | bytes 14155776 | tf_op jit(solution)/shard_map/all_to_all | solution.py:117
  198.5 54.4 %all-to-all-start.3 = ((f32[32,4,4,2]{2,3,1,0:T(2,128)}), f32[32,4,4,2]{2,3,1,0:T(2,128)S(1)}, u32[]{:S(2)}, u32[]{:S(2)}) async-start(f32[32,4,4,2]{2,3,1,0:T(2,128)} %copy.143), calls=%async_computation.3 | async-start | bytes 262144 | tf_op jit(solution)/shard_map/all_to_all | solution.py:142
  252.9 24.7 %all-to-all-start.1 = ((f32[32,4,4,320]{3,2,1,0:T(4,128)}), f32[32,4,4,320]{3,2,1,0:T(4,128)S(1)}, u32[]{:S(2)}, u32[]{:S(2)}) async-start(f32[32,4,4,320]{3,2,1,0:T(4,128)} %copy.136), calls=%async_computation.1 | async-start | bytes 1572864 | tf_op jit(solution)/shard_map/all_to_all | solution.py:141
  307.3 29.6 %copy-start.1 = (bf16[32,4,2304]{2,1,0:T(4,128)(2,1)S(1)}, bf16[32,4,2304]{2,1,0:T(4,128)(2,1)}, u32[]{:S(2)}) copy-start(bf16[32,4,2304]{2,1,0:T(4,128)(2,1)} %param.10) | copy-start | bytes 1769476
where the time goes:
time: 338 us; the launch traced here: 337 us
  blocking collectives  153 us (45%)
  other arithmetic  54 us (16%)
  starting transfers between devices  47.1 us (14%)
  local copies, waits for them, and re-layouts  42.4 us (13%)
  matrix products  21.1 us (6%)
  waiting for transfers between devices  18.3 us (5%)
    all_gather x1, blocking collectives, on_device(): taps_all = lax.all_gather(conv_weight, 'heads', axis=1, tiled=True)  141 us
    all_to_all x1, starting transfers between devices, on_device(): lax.all_to_all(gate_pre, 'heads', split_axis=0, concat_axis=2, tiled=True)  27.5 us
    reduce_sum x2, other arithmetic, run_steps(): heads_now = jnp.sum(queries[:, step_index, :, :, None] * updated, axis=2)  22 us
    reduce_sum x3, other arithmetic, run_steps(): predicted = jnp.sum(keys_all[:, step_index, :, :, None] * faded, axis=2)  18.7 us
    all_to_all x1, waiting for transfers between devices, on_device(): lax.all_to_all(projected, 'heads', split_axis=0, concat_axis=2, tiled=True)  18.3 us
    all_to_all x1, blocking collectives, on_device(): lax.all_to_all(local_out, 'heads', split_axis=2, concat_axis=0, tiled=True)  12.1 us
    reshape x1, local copies, waits for them, and re-layouts, on_device(): mine_weight.reshape(D, per_device * unit_width)  11.9 us
    dot_general x1, matrix products, pick_state(): jnp.einsum('rhkv,uh->rukv', delta_state, selector, precision=lax.Precisio...  11.6 us
  transfers between devices with their start and end apart: 4, of which 1 were waited for; matrix products, arithmetic and copies ran while one was open for 20% of the time, Pallas kernels for 0%

commit v1 on v0

--- a/solution.py
+++ b/solution.py
@@ -138,7 +138,12 @@
     tap_table = select_units(taps_all, selector_low, halves, False)
     rows_dev = delta_state.shape[0]
     got_projected, got_gate = (
-        lax.all_to_all(projected, "heads", split_axis=0, concat_axis=2, tiled=True),
+        jnp.concatenate(
+            lax.all_to_all(
+                jnp.stack(jnp.split(projected, lax.axis_size("heads"), axis=0)), "heads", 0, 0
+            ),
+            axis=2,
+        ),
         lax.all_to_all(gate_pre, "heads", split_axis=0, concat_axis=2, tiled=True),
     )
     live_lengths = lax.dynamic_slice_in_dim(lengths_old, my_index * rows_dev, rows_dev, 0)

time: 338 us -> 338 us (level)
    dot_general x2 -> x0, local copies, waits for them, and re-layouts: 10.3 us -> none  [on_device(): jnp.dot(flattened, mine_weight.reshape(D, per_device * unit_width), prefe...]
    unnamed x16 -> x31, local copies, waits for them, and re-layouts: 3.04 us -> 12.5 us
where the time goes in v1:
time: 338 us; the launch traced here: 337 us
  blocking collectives  152 us (45%)
  other arithmetic  54 us (16%)
  starting transfers between devices  47.1 us (14%)
  local copies, waits for them, and re-layouts  44.2 us (13%)
  matrix products  20 us (6%)
  waiting for transfers between devices  18.3 us (5%)
    all_gather x1, blocking collectives, on_device(): taps_all = lax.all_gather(conv_weight, 'heads', axis=1, tiled=True)  140 us
    all_to_all x1, starting transfers between devices, on_device(): lax.all_to_all(gate_pre, 'heads', split_axis=0, concat_axis=2, tiled=True)  27.5 us
    reduce_sum x2, other arithmetic, run_steps(): heads_now = jnp.sum(queries[:, step_index, :, :, None] * updated, axis=2)  22 us
    reduce_sum x3, other arithmetic, run_steps(): predicted = jnp.sum(keys_all[:, step_index, :, :, None] * faded, axis=2)  18.7 us
    all_to_all x1, waiting for transfers between devices, on_device(): lax.all_to_all(jnp.stack(jnp.split(projected, lax.axis_size('heads'), axi...  18.3 us
    unnamed x31, local copies, waits for them, and re-layouts  12.5 us
    all_to_all x1, blocking collectives, on_device(): lax.all_to_all(local_out, 'heads', split_axis=2, concat_axis=0, tiled=True)  12.1 us
    reshape x1, local copies, waits for them, and re-layouts, on_device(): mine_weight.reshape(D, per_device * unit_width)  11.9 us
  transfers between devices with their start and end apart: 4, of which 1 were waited for; matrix products, arithmetic and copies ran while one was open for 20% of the time, Pallas kernels for 0%

profile of v1, /device:TPU:0, one launch (start us, length us, event | category | flops | bytes accessed | tf_op | source)
XLA Modules:
  0.0 336.6 jit_solution(13988463778477545711)
XLA Ops:
  0.0 0.7 and_select_fusion.1
  0.7 0.7 select_reduce_fusion.1
  1.6 1.0 fusion.8
  2.5 0.7 copy.228
  3.2 7.4 %all-to-all-start.2 = ((bf16[144,16,4,2]{0,3,2,1:T(2,128)(2,1)}), bf16[144,16,4,2]{0,3,2,1:T(2,128)(2,1)S(1)}, u32[]{:S(2)}, u32[]{:S(2)}) async-start(bf16[144,16,4,2]{0,3,2,1:T(2,128)(2,1)} %bitcast.34), calls=%async_computation.2 | async-start | bytes 131072 | tf_op jit(solution)/shard_map/all_to_all | solution.py:118
  10.7 0.7 fusion.50
  11.3 2.7 copy.232
  14.1 2.0 convert_bitcast_fusion
  16.1 2.5 fusion.52
  18.6 0.8 slice_select_fusion.1
  19.4 6.9 %pad_maximum_fusion = bf16[144,16,4,320]{3,2,1,0:T(4,128)(2,1)} fusion(bf16[144,16,4,64]{3,2,1,0:T(4,128)(2,1)S(1)} %bitcast.155, bf16[144,16,4,128]{3,2,1,0:T(4,128)(2,1)S(1)} %bitcast.154, bf16[144,16,4,128]{3,2,1,0:T(4,128)(2,1)S(1)} %bitcast.153), kind=kLoop, calls=%fused_computation.15 | loop fusion | flops 17694720 | bytes 11796480 | tf_op jit(solution)/shard_map/concatenate | solution.py:42
  26.3 9.1 %copy.227 = bf16[144,16,4,320]{3,2,0,1:T(4,128)(2,1)} copy(bf16[144,16,4,320]{3,2,1,0:T(4,128)(2,1)} %pad_maximum_fusion) | data formatting | bytes 11796480 | tf_op jit(solution)/shard_map/concatenate | solution.py:42
  35.4 6.2 %all-to-all-start = ((bf16[144,16,4,320]{3,2,0,1:T(4,128)(2,1)}), bf16[144,16,4,320]{3,2,0,1:T(4,128)(2,1)}, u32[]{:S(2)}, u32[]{:S(2)}) async-start(bf16[144,16,4,320]{3,2,0,1:T(4,128)(2,1)} %copy.227), calls=%async_computation | async-start | bytes 14155776 | tf_op jit(solution)/shard_map/all_to_all | solution.py:117
  42.1 0.5 copy.177
  42.7 140.3 %all_gather.3 = bf16[4,12288]{1,0:T(4,128)(2,1)S(1)} all-gather(bf16[4,768]{1,0:T(4,128)(2,1)S(1)} %copy-done.3), channel_id=1, replica_groups=mesh['groups'=2,'heads'=16] {'heads'}, dimensions={1}, use_global_device_ids=true | all-gather | bytes 104448 | tf_op jit(solution)/shard_map/all_gather | solution.py:137
  183.3 0.5 convolution_bitcast_fusion
  185.0 11.6 %fusion.4 = f32[2,64,128,128]{3,1,2,0:T(8,128)} fusion(f32[2,32,128,128]{3,2,1,0:T(8,128)} %param.14, s32[64]{0:T(128)S(1)} %select_reduce_fusion), kind=kOutput, calls=%fused_computation.20 | convolution fusion | flops 805308416 | bytes 12583168 | tf_op jit(solution)/shard_map/rhkv,uh->rukv/dot_general | solution.py:46
  196.7 0.5 fusion.17
  197.2 0.8 copy.203
  198.0 27.5 %all-to-all-start.3 = ((f32[32,4,4,2]{2,3,1,0:T(2,128)}), f32[32,4,4,2]{2,3,1,0:T(2,128)S(1)}, u32[]{:S(2)}, u32[]{:S(2)}) async-start(f32[32,4,4,2]{2,3,1,0:T(2,128)} %copy.203), calls=%async_computation.3 | async-start | bytes 262144 | tf_op jit(solution)/shard_map/all_to_all | solution.py:147
  225.5 11.9 %reshape.227 = bf16[2304,1280]{1,0:T(8,128)(2,1)} reshape(bf16[16,144,1,4,320]{4,3,1,0,2:T(4,128)(2,1)} %bitcast.22) | data formatting | bytes 11796480 | tf_op jit(solution)/shard_map/reshape | solution.py:131
  237.4 3.6 %fusion.59 = f32[128,1280]{1,0:T(8,128)S(1)} fusion(bf16[128,2304]{1,0:T(8,128)(2,1)S(1)} %reshape.225, bf16[2304,1280]{1,0:T(8,128)(2,1)} %reshape.227), kind=kOutput, calls=%fused_computation.141 | convolution fusion | flops 754974720 | bytes 7143424 | tf_op jit(solution)/shard_map/dot_general | solution.py:129
  241.2 0.6 copy_dynamic-update-slice_fusion.15
  243.3 0.6 copy_dynamic-update-slice_fusion.14
  243.9 0.6 copy_dynamic-update-slice_fusion.13
  244.6 0.6 copy_dynamic-update-slice_fusion.12
  245.2 0.6 copy_dynamic-update-slice_fusion.11
  245.8 0.6 copy_dynamic-update-slice_fusion.10
  246.4 0.6 copy_dynamic-update-slice_fusion.9
  247.1 0.6 copy_dynamic-update-slice_fusion.8
  247.7 0.6 copy_dynamic-update-slice_fusion.7
  248.3 0.6 copy_dynamic-update-slice_fusion.6
  249.0 0.6 copy_dynamic-update-slice_fusion.5
  249.6 0.6 copy_dynamic-update-slice_fusion.4
  250.2 0.6 copy_dynamic-update-slice_fusion.3
  250.8 0.6 copy_dynamic-update-slice_fusion.2
  251.5 0.6 copy_dynamic-update-slice_fusion.1
  252.1 0.6 copy_dynamic-update-slice_fusion
  252.7 6.0 %all-to-all-start.1 = ((f32[16,2,4,4,320]{4,2,3,1,0:T(4,128)}), f32[16,2,4,4,320]{4,2,3,1,0:T(4,128)S(1)}, u32[]{:S(2)}, u32[]{:S(2)}) async-start(f32[16,2,4,4,320]{4,2,3,1,0:T(4,128)} %copy_dynamic-update-slice_fusion), calls=%async_computation.1 | async-start | bytes 1572864 | tf_op jit(solution)/shard_map/all_to_all | solution.py:142
  259.1 18.3 %all-to-all-done.1 = f32[16,2,4,4,320]{4,2,3,1,0:T(4,128)S(1)} async-done(((f32[16,2,4,4,320]{4,2,3,1,0:T(4,128)}), f32[16,2,4,4,320]{4,2,3,1,0:T(4,128)S(1)}, u32[]{:S(2)}, u32[]{:S(2)}) %all-to-all-start.1) | async-done | bytes 655392 | tf_op jit(solution)/shard_map/all_to_all | solution.py:142
  277.5 1.5 divide_multiply_fusion
  281.9 8.5 %multiply_reduce_fusion.7 = (f32[2,64,64]{2,1,0:T(8,128)S(1)}, f32[2,64,128,64]{3,1,2,0:T(8,128)S(1)}) fusion(f32[2,64,128]{1,2,0:T(8,128)S(1)} %copy.208, f32[2,64]{1,0:T(2,128)S(1)} %bitcast.187, f32[2,64,128,128]{3,1,2,0:T(8,128)} %fusion.4, pred[64]{0:T(512)(128)(4,1)S(1)} %fusion.50), kind=kLoop, calls=%fused_computation.12 | loop fusion | flops 4186112 | bytes 12681792 | tf_op jit(solution)/shard_map/reduce_sum | solution.py:73
  290.4 5.1 %multiply_reduce_fusion.5 = f32[2,64,64]{2,1,0:T(8,128)S(1)} fusion(f32[2,64,128,64]{3,1,2,0:T(8,128)S(1)} %get-tuple-element.16, f32[2,64,128]{1,2,0:T(8,128)S(1)} %copy.211, f32[2,64]{1,0:T(2,128)S(1)} %bitcast.194, f32[2,64,64]{2,1,0:T(8,128)S(1)} %sub.35, f32[2,64,128]{1,2,0:T(8,128)S(1)} %copy.207, f32[2,64]{1,0:T(2,128)S(1)} %bitcast.188, ...), kind=kLoop, calls=%fused_computation.9 | loop fusion | flops 7331840 | bytes 4391938 | tf_op jit(solution)/shard_map/reduce_sum | solution.py:73
  295.5 11.4 %multiply_reduce_fusion.6 = (bf16[2,64,64]{2,1,0:T(8,128)(2,1)S(1)}, bf16[2,64,64]{2,1,0:T(8,128)(2,1)S(1)}, f32[2,64,64]{2,1,0:T(8,128)S(1)}, f32[2,64,128,64]{3,1,2,0:T(8,128)S(1)}) fusion(f32[2,64,128,64]{3,1,2,0:T(8,128)S(1)} %get-tuple-element.16, f32[2,64,64]{2,1,0:T(8,128)S(1)} %sub.35, f32[2,64,128]{1,2,0:T(8,128)S(1)} %copy.207, ...), kind=kLoop, calls=%fused_computation.10 | loop fusion | flops 15704064 | bytes 8848900 | tf_op jit(solution)/shard_map/reduce_sum | solution.py:80
  307.0 5.1 %multiply_reduce_fusion.1 = f32[2,64,64]{2,1,0:T(8,128)S(1)} fusion(f32[2,64,128,64]{3,1,2,0:T(8,128)S(1)} %get-tuple-element.18, f32[2,64,128]{1,2,0:T(8,128)S(1)} %copy.217, f32[2,64]{1,0:T(2,128)S(1)} %bitcast.192, f32[2,64,64]{2,1,0:T(8,128)S(1)} %sub.37, f32[2,64,128]{1,2,0:T(8,128)S(1)} %copy.213, f32[2,64]{1,0:T(2,128)S(1)} %bitcast.185, ...), kind=kLoop, calls=%fused_computation.2 | loop fusion | flops 7331840 | bytes 4391938 | tf_op jit(solution)/shard_map/reduce_sum | solution.py:73
  312.1 10.5 %multiply_reduce_fusion.2 = (bf16[2,64,64]{2,1,0:T(8,128)(2,1)S(1)}, bf16[2,64,64]{2,1,0:T(8,128)(2,1)S(1)}) fusion(f32[2,64,128,64]{3,1,2,0:T(8,128)S(1)} %get-tuple-element.18, f32[2,64,64]{2,1,0:T(8,128)S(1)} %sub.37, f32[2,64,128]{1,2,0:T(8,128)S(1)} %copy.213, f32[2,64]{1,0:T(2,128)S(1)} %bitcast.186, f32[2,64,128]{1,2,0:T(8,128)S(1)} %copy.212, ...), kind=kLoop, calls=%fused_computation.4 | loop fusion | flops 11517952 | bytes 4555778 | tf_op jit(solution)/shard_map/reduce_sum | solution.py:80
  323.3 12.1 %all_to_all.68 = bf16[16,2,1024]{2,1,0:T(2,128)(2,1)S(1)} all-to-all(bf16[16,2,1024]{2,1,0:T(2,128)(2,1)S(1)} %reshape.241), channel_id=1, replica_groups=mesh['groups'=2,'heads'=16] {'heads'}, dimensions={0} | all-to-all | bytes 131072 | tf_op jit(solution)/shard_map/all_to_all | solution.py:153
  335.9 0.7 copy.221
  (98 shorter events, 8.2 us)
Async XLA Ops:
  0.0 41.6 %copy-start = (bf16[32,4,2304]{2,1,0:T(4,128)(2,1)S(1)}, bf16[32,4,2304]{2,1,0:T(4,128)(2,1)}, u32[]{:S(2)}) copy-start(bf16[32,4,2304]{2,1,0:T(4,128)(2,1)} %param.10) | copy-start | bytes 1769476
  3.2 32.2 %all-to-all-start.2 = ((bf16[144,16,4,2]{0,3,2,1:T(2,128)(2,1)}), bf16[144,16,4,2]{0,3,2,1:T(2,128)(2,1)S(1)}, u32[]{:S(2)}, u32[]{:S(2)}) async-start(bf16[144,16,4,2]{0,3,2,1:T(2,128)(2,1)} %bitcast.34), calls=%async_computation.2 | async-start | bytes 131072 | tf_op jit(solution)/shard_map/all_to_all | solution.py:118
  35.4 6.2 %copy-start.4 = (s32[32]{0:T(128)S(1)}, s32[32]{0:T(128)}, u32[]{:S(2)}) copy-start(s32[32]{0:T(128)} %param.18) | copy-start | bytes 388
  35.4 7.3 %copy-start.3 = (bf16[4,768]{1,0:T(4,128)(2,1)S(1)}, bf16[4,768]{1,0:T(4,128)(2,1)}, u32[]{:S(2)}) copy-start(bf16[4,768]{1,0:T(4,128)(2,1)} %param.13) | copy-start | bytes 18436
  35.4 147.6 %copy-start.2 = (f32[2,3,12288]{2,0,1:T(2,128)S(1)}, f32[2,3,12288]{2,0,1:T(2,128)}, u32[]{:S(2)}) copy-start(f32[2,3,12288]{2,0,1:T(2,128)} %param.15) | copy-start | bytes 884740
  35.4 149.0 %copy-start.5 = (s32[32]{0:T(128)S(1)}, s32[32]{0:T(128)}, u32[]{:S(2)}) copy-start(s32[32]{0:T(128)} %param.19) | copy-start | bytes 388
  35.4 162.6 %all-to-all-start = ((bf16[144,16,4,320]{3,2,0,1:T(4,128)(2,1)}), bf16[144,16,4,320]{3,2,0,1:T(4,128)(2,1)}, u32[]{:S(2)}, u32[]{:S(2)}) async-start(bf16[144,16,4,320]{3,2,0,1:T(4,128)(2,1)} %copy.227), calls=%async_computation | async-start | bytes 14155776 | tf_op jit(solution)/shard_map/all_to_all | solution.py:117
  198.0 54.7 %all-to-all-start.3 = ((f32[32,4,4,2]{2,3,1,0:T(2,128)}), f32[32,4,4,2]{2,3,1,0:T(2,128)S(1)}, u32[]{:S(2)}, u32[]{:S(2)}) async-start(f32[32,4,4,2]{2,3,1,0:T(2,128)} %copy.203), calls=%async_computation.3 | async-start | bytes 262144 | tf_op jit(solution)/shard_map/all_to_all | solution.py:147
  252.7 24.7 %all-to-all-start.1 = ((f32[16,2,4,4,320]{4,2,3,1,0:T(4,128)}), f32[16,2,4,4,320]{4,2,3,1,0:T(4,128)S(1)}, u32[]{:S(2)}, u32[]{:S(2)}) async-start(f32[16,2,4,4,320]{4,2,3,1,0:T(4,128)} %copy_dynamic-update-slice_fusion), calls=%async_computation.1 | async-start | bytes 1572864 | tf_op jit(solution)/shard_map/all_to_all | solution.py:142
  307.0 29.6 %copy-start.1 = (bf16[32,4,2304]{2,1,0:T(4,128)(2,1)S(1)}, bf16[32,4,2304]{2,1,0:T(4,128)(2,1)}, u32[]{:S(2)}) copy-start(bf16[32,4,2304]{2,1,0:T(4,128)(2,1)} %param.10) | copy-start | bytes 1769476
